TPU v7x, 128 devices: a whole 4x4x4 slice. The times are simulated.
128 devices in a mesh: dp: 16 (over y, x), seq: 8 (over z, core).
Axes of the slice: x: 4, y: 4, z: 4, core: 2. Of those that a mesh axis runs over, the one named last changes fastest.
Arguments:
- feats: bfloat16 [65536, 1024], P(('dp', 'seq')), may hold values from -6 to 6
- gain: float32 [1024], replicated, may hold values from 0.1 to 1.9
- w_qkv: bfloat16 [1024, 3072], replicated, as said below
- w_out: bfloat16 [1024, 1024], replicated, may hold values from -3 to 3
- block_cols: int32 [16, 32, 8], P('dp'), may hold values from 0 to 31, as said below
- block_counts: int32 [16, 32], P('dp'), may hold values from 1 to 8, 128 in all within a row
- cotan: bfloat16 [65536, 1024], P(('dp', 'seq')), may hold values from -0.3984375 to 0.3984375
Outputs:
- result: bfloat16 [65536, 1024], P(('dp', 'seq'))
- grad_feats: bfloat16 [65536, 1024], P(('dp', 'seq'))
- grad_qkv: bfloat16 [1024, 3072], P('seq')
- grad_out: bfloat16 [1024, 1024], P('seq')
Inputs may be any that keep to these rules, and one draw needn't show every extreme that they name: `block_cols`: for every batch and row block r, the 8 listed column blocks are distinct and the first is r itself. `block_counts`: each batch's counts sum to 128. `w_qkv`: entries lie within 70 / sqrt(1024) in magnitude.
All inputs are finite; a program needn't handle non-finite values.
Results may differ from a plain program's by a relative error of at most 0.014.
Values may be sent and summed in bfloat16 or wider, within the bound.
A program may use at most 128 MiB of HBM per device.

v0:
```python
import jax
import jax.numpy as jnp
from jax import lax
from jax.sharding import PartitionSpec as P

HD = 64
BLK = 128
MAXB = 8
EPSILON = 1e-05


def layer_norm(feats, gain):
    values_f = feats.astype(jnp.float32)
    centred = values_f - jnp.mean(values_f, axis=1, keepdims=True)
    inverse = lax.rsqrt(jnp.mean(centred * centred, axis=1, keepdims=True) + EPSILON)
    scaled = centred * inverse
    return (scaled, inverse, (scaled * gain[None, :]).astype(jnp.bfloat16))


def live_slots(counts):
    return jnp.arange(MAXB, dtype=jnp.int32)[None, :] < counts[:, None]


def contract_rows(left_cols, right_cols):
    return lax.dot_general(
        left_cols, right_cols, (((0,), (0,)), ((), ())), preferred_element_type=jnp.float32
    )


def stacked_table(key_heads, value_heads, block_total, head_count):
    key_b = key_heads.reshape(block_total, BLK, head_count, HD)
    value_b = value_heads.reshape(block_total, BLK, head_count, HD)
    return jnp.concatenate([key_b, value_b], axis=3).reshape(block_total, BLK * head_count * 2 * HD)


def select_blocks(onehot, table, head_count):
    picked = jnp.einsum("gsc,cf->gsf", onehot, table, preferred_element_type=jnp.float32).astype(
        jnp.bfloat16
    )
    picked = picked.reshape(onehot.shape[0], onehot.shape[1], BLK, head_count, 2 * HD)
    return (picked[..., :HD], picked[..., HD:])


def forward_blocks(query_heads, key_heads, value_heads, col_blocks, counts, head_count):
    per_step = 4
    block_total = query_heads.shape[0] // BLK
    steps_count = block_total // per_step
    query_b = query_heads.reshape(steps_count, per_step, BLK, head_count, HD)
    table = stacked_table(key_heads, value_heads, block_total, head_count)
    col_steps = col_blocks.reshape(steps_count, per_step, MAXB)
    count_steps = counts.reshape(steps_count, per_step)
    block_range = jnp.arange(block_total, dtype=jnp.int32)
    score_scale = HD ** (-0.5)

    def forward_block_step(inputs):
        query_g, col_g, count_g = inputs
        onehot = (col_g[:, :, None] == block_range[None, None, :]).astype(jnp.bfloat16)
        key_g, value_g = select_blocks(onehot, table, head_count)
        scores = (
            jnp.einsum("gqhd,gskhd->ghqsk", query_g, key_g, preferred_element_type=jnp.float32)
            * score_scale
        )
        live_mask = live_slots(count_g)[:, None, None, :, None]
        row_max = jnp.max(jnp.where(live_mask, scores, -jnp.inf), axis=(3, 4), keepdims=True)
        row_total = jnp.sum(
            jnp.where(live_mask, jnp.exp(scores - row_max), 0.0), axis=(3, 4), keepdims=True
        )
        log_total = row_max + jnp.log(row_total)
        probabilities = jnp.where(live_mask, jnp.exp(scores - log_total), 0.0).astype(jnp.bfloat16)
        attended = jnp.einsum(
            "ghqsk,gskhd->gqhd", probabilities, value_g, preferred_element_type=jnp.float32
        )
        return (attended.astype(jnp.bfloat16), log_total[:, :, :, 0, 0])

    attended, log_total = lax.map(forward_block_step, (query_b, col_steps, count_steps))
    return (attended.reshape(query_heads.shape), log_total)


def backward_blocks(
    query_heads,
    key_heads,
    value_heads,
    attended_heads,
    grad_heads,
    log_total,
    col_blocks,
    counts,
    head_count,
):
    per_step = 4
    block_total = query_heads.shape[0] // BLK
    steps_count = block_total // per_step
    query_b = query_heads.reshape(steps_count, per_step, BLK, head_count, HD)
    grad_b = grad_heads.reshape(steps_count, per_step, BLK, head_count, HD)
    attended_b = attended_heads.reshape(steps_count, per_step, BLK, head_count, HD)
    table = stacked_table(key_heads, value_heads, block_total, head_count)
    col_steps = col_blocks.reshape(steps_count, per_step, MAXB)
    count_steps = counts.reshape(steps_count, per_step)
    delta_all = jnp.sum(attended_b.astype(jnp.float32) * grad_b.astype(jnp.float32), axis=4)
    block_range = jnp.arange(block_total, dtype=jnp.int32)
    score_scale = HD ** (-0.5)

    def backward_block_step(carry, inputs):
        key_sum, value_sum = carry
        query_g, grad_g, delta_g, log_g, col_g, count_g = inputs
        matches = col_g[:, :, None] == block_range[None, None, :]
        key_g, value_g = select_blocks(matches.astype(jnp.bfloat16), table, head_count)
        scores = (
            jnp.einsum("gqhd,gskhd->ghqsk", query_g, key_g, preferred_element_type=jnp.float32)
            * score_scale
        )
        live_mask = live_slots(count_g)[:, None, None, :, None]
        probabilities = jnp.where(
            live_mask, jnp.exp(scores - log_g[:, :, :, None, None]), 0.0
        ).astype(jnp.bfloat16)
        prob_grad = jnp.einsum(
            "gqhd,gskhd->ghqsk", grad_g, value_g, preferred_element_type=jnp.float32
        )
        delta_t = jnp.transpose(delta_g, (0, 2, 1))[:, :, :, None, None]
        score_grad = (
            probabilities.astype(jnp.float32) * (prob_grad - delta_t) * score_scale
        ).astype(jnp.bfloat16)
        query_grad = jnp.einsum(
            "ghqsk,gskhd->gqhd", score_grad, key_g, preferred_element_type=jnp.float32
        ).astype(jnp.bfloat16)
        key_pairs = jnp.einsum(
            "ghqsk,gqhd->gskhd", score_grad, query_g, preferred_element_type=jnp.float32
        )
        value_pairs = jnp.einsum(
            "ghqsk,gqhd->gskhd", probabilities, grad_g, preferred_element_type=jnp.float32
        )
        selector = matches.astype(jnp.float32)
        key_sum = key_sum + jnp.einsum(
            "gsc,gskhd->ckhd", selector, key_pairs, precision=lax.Precision.HIGHEST
        )
        value_sum = value_sum + jnp.einsum(
            "gsc,gskhd->ckhd", selector, value_pairs, precision=lax.Precision.HIGHEST
        )
        return ((key_sum, value_sum), query_grad)

    zeros_f = jnp.zeros((block_total, BLK, head_count, HD), jnp.float32)
    (key_sum, value_sum), query_grad = lax.scan(
        backward_block_step,
        (zeros_f, zeros_f),
        (query_b, grad_b, delta_all, log_total, col_steps, count_steps),
    )
    shape = query_heads.shape
    return (
        query_grad.reshape(shape),
        key_sum.reshape(shape).astype(jnp.bfloat16),
        value_sum.reshape(shape).astype(jnp.bfloat16),
    )


def body(feats, gain, w_qkv, w_out, block_cols, block_counts, cotan):
    seq_count = lax.axis_size("seq")
    model_width = feats.shape[1]
    qkv_width = 3 * model_width
    scaled, inverse, normed = layer_norm(feats, gain)
    mixed_proj = jnp.dot(normed, w_qkv, preferred_element_type=jnp.float32).astype(jnp.bfloat16)
    query_rows = mixed_proj[:, :model_width]
    key_rows = mixed_proj[:, model_width : 2 * model_width]
    value_rows = mixed_proj[:, 2 * model_width :]
    query_heads, key_heads, value_heads = (
        lax.all_to_all(query_rows, "seq", split_axis=1, concat_axis=0, tiled=True),
        lax.all_to_all(key_rows, "seq", split_axis=1, concat_axis=0, tiled=True),
        lax.all_to_all(value_rows, "seq", split_axis=1, concat_axis=0, tiled=True),
    )
    head_count = query_heads.shape[1] // HD
    col_blocks = block_cols[0]
    counts = block_counts[0]
    attended_heads, log_total = forward_blocks(
        query_heads, key_heads, value_heads, col_blocks, counts, head_count
    )
    attended = lax.all_to_all(attended_heads, "seq", split_axis=0, concat_axis=1, tiled=True)
    result = (
        feats.astype(jnp.float32) + jnp.dot(attended, w_out, preferred_element_type=jnp.float32)
    ).astype(jnp.bfloat16)
    grad_att = lax.dot_general(
        cotan, w_out, (((1,), (1,)), ((), ())), preferred_element_type=jnp.float32
    ).astype(jnp.bfloat16)
    grad_heads = lax.all_to_all(grad_att, "seq", split_axis=1, concat_axis=0, tiled=True)
    query_grad, key_grad, value_grad = backward_blocks(
        query_heads,
        key_heads,
        value_heads,
        attended_heads,
        grad_heads,
        log_total,
        col_blocks,
        counts,
        head_count,
    )
    query_back, key_back, value_back = (
        lax.all_to_all(query_grad, "seq", split_axis=0, concat_axis=1, tiled=True),
        lax.all_to_all(key_grad, "seq", split_axis=0, concat_axis=1, tiled=True),
        lax.all_to_all(value_grad, "seq", split_axis=0, concat_axis=1, tiled=True),
    )
    grad_mixed = jnp.concatenate([query_back, key_back, value_back], axis=1)
    grad_normed = lax.dot_general(
        grad_mixed, w_qkv, (((1,), (1,)), ((), ())), preferred_element_type=jnp.float32
    )
    gained = grad_normed * gain[None, :]
    mean_one = jnp.mean(gained, axis=1, keepdims=True)
    mean_two = jnp.mean(gained * scaled, axis=1, keepdims=True)
    grad_feats = (
        cotan.astype(jnp.float32) + inverse * (gained - mean_one - scaled * mean_two)
    ).astype(jnp.bfloat16)
    summed = lax.psum(
        jnp.concatenate(
            [contract_rows(normed, grad_mixed), contract_rows(attended, cotan)], axis=1
        ),
        ("dp", "seq"),
    )
    shard_rows = model_width // seq_count
    own_rows = lax.dynamic_slice_in_dim(summed, lax.axis_index("seq") * shard_rows, shard_rows, 0)
    grad_qkv = own_rows[:, :qkv_width].astype(jnp.bfloat16)
    grad_out = own_rows[:, qkv_width:].astype(jnp.bfloat16)
    return (result, grad_feats, grad_qkv, grad_out)


def solution(mesh):
    in_specs = (
        P(("dp", "seq"), None),
        P(),
        P(),
        P(),
        P("dp", None, None),
        P("dp", None),
        P(("dp", "seq"), None),
    )
    out_specs = (P(("dp", "seq"), None), P(("dp", "seq"), None), P("seq", None), P("seq", None))
    return jax.shard_map(body, mesh=mesh, in_specs=in_specs, out_specs=out_specs, check_vma=False)
```

profile of v0, /device:TPU:0, one launch (start us, length us, event | category | flops | bytes accessed | tf_op | source)
XLA Modules:
  0.0 628.2 jit_solution(8621975070728321357)
XLA Ops:
  4.0 6.7 %convolution_convert_fusion.2 = bf16[512,3072]{1,0:T(8,128)(2,1)S(1)} fusion(bf16[1024,3072]{1,0:T(8,128)(2,1)} %param.13, bf16[512,1024]{1,0:T(8,128)(2,1)S(1)} %copy-done.8, f32[1024]{0:T(1024)S(1)} %copy-done.19, f32[512]{0:T(512)S(1)} %add_rsqrt_fusion, f32[512]{0:T(512)S(1)} %broadcast_multiply_fusion.2), kind=kOutput, calls=%fused_computation.70 | convolution fusion | flops 3225419776 | bytes 10493952 | tf_op jit(solution)/shard_map/dot_general | solution.py:160
  13.7 5.4 all-to-all-start.1
  21.4 13.7 %all-to-all-done.1 = bf16[512,8,128]{0,2,1:T(8,128)(2,1)S(1)} async-done(((bf16[512,8,128]{0,2,1:T(8,128)(2,1)}), bf16[512,8,128]{0,2,1:T(8,128)(2,1)S(1)}, u32[]{:S(2)}, u32[]{:S(2)}) %all-to-all-start.1) | async-done | bytes 1048608 | tf_op jit(solution)/shard_map/all_to_all | solution.py:167
  35.0 4.2 all-to-all-start
  41.6 13.7 %all-to-all-done = bf16[512,8,128]{0,2,1:T(8,128)(2,1)} async-done(((bf16[512,8,128]{0,2,1:T(8,128)(2,1)}), bf16[512,8,128]{0,2,1:T(8,128)(2,1)}, u32[]{:S(2)}, u32[]{:S(2)}) %all-to-all-start) | async-done | bytes 1048608 | tf_op jit(solution)/shard_map/all_to_all | solution.py:166
  55.2 4.2 all-to-all-start.2
  60.9 3.5 convolution_convert_fusion.3
  74.0 3.1 pad_maximum_fusion.2
  77.0 4.7 copy.69
  81.7 4.5 reshape.177
  86.2 5.2 all-to-all-start.4
  94.5 59.6 %while.28 = (s32[]{:T(128)}, bf16[8,4,128,2,64]{2,1,4,3,0:T(4,128)(2,1)S(1)}, f32[8,4,2,128]{3,2,1,0:T(2,128)S(1)}, s32[8,4,8]{2,1,0:T(4,128)S(1)}, bf16[32,3276...) while((s32[]{:T(128)}, ...), condition=%wide.region_5.6_spmd.clone, body=%wide.region_2.5_spmd.clone.sunk | while | flops 348192800 | bytes 23626400 | solution.py:75
  155.3 4.8 all-to-all-start.3
  165.6 239.2 %while.29 = (s32[]{:T(128)}, f32[32,128,2,64]{1,0,3,2:T(8,128)}, f32[32,128,2,64]{1,0,3,2:T(8,128)}, bf16[8,4,128,2,64]{2,1,4,3,0:T(4,128)(2,1)}, s32[8,4,8]{2,1...) while((s32[]{:T(128)}, f32[32,128,2,64]{1,0,3,2:T(8,128)}, ...), condition=%wide.region_8.9_spmd.clone, body=%wide.region_7.8_spmd.clone.sunk | while | flops 1153502208 | bytes 98731120 | solution.py:142
  168.1 3.0 fusion.129
  182.9 5.5 bitcast_add_fusion.4
  189.9 3.5 bitcast_add_fusion.5
  197.4 3.0 fusion.129
  212.2 6.1 bitcast_add_fusion.4
  219.9 3.5 bitcast_add_fusion.5
  227.3 3.0 fusion.129
  242.1 6.1 bitcast_add_fusion.4
  249.8 3.5 bitcast_add_fusion.5
  257.3 3.0 fusion.129
  272.0 6.1 bitcast_add_fusion.4
  279.7 3.5 bitcast_add_fusion.5
  287.2 3.0 fusion.129
  302.0 6.1 bitcast_add_fusion.4
  309.7 3.5 bitcast_add_fusion.5
  317.1 3.0 fusion.129
  331.9 6.1 bitcast_add_fusion.4
  339.6 3.5 bitcast_add_fusion.5
  361.8 6.1 bitcast_add_fusion.4
  369.5 3.5 bitcast_add_fusion.5
  391.8 6.1 bitcast_add_fusion.4
  399.4 3.5 bitcast_add_fusion.5
  410.6 4.8 all-to-all-start.7
  421.3 10.2 %all-to-all-done.7 = bf16[8,512,128]{1,2,0:T(8,128)(2,1)} async-done(((bf16[8,512,128]{1,2,0:T(8,128)(2,1)}), bf16[8,512,128]{1,2,0:T(8,128)(2,1)}, u32[]{:S(2)}, u32[]{:S(2)}) %all-to-all-start.7) | async-done | bytes 1048608 | tf_op jit(solution)/shard_map/all_to_all | solution.py:197
  431.5 4.2 all-to-all-start.6
  437.0 14.7 %all-to-all-done.6 = bf16[8,512,128]{1,2,0:T(8,128)(2,1)} async-done(((bf16[8,512,128]{1,2,0:T(8,128)(2,1)}), bf16[8,512,128]{1,2,0:T(8,128)(2,1)}, u32[]{:S(2)}, u32[]{:S(2)}) %all-to-all-start.6) | async-done | bytes 1048608 | tf_op jit(solution)/shard_map/all_to_all | solution.py:196
  451.7 4.2 all-to-all-start.5
  456.0 4.8 fusion.76
  460.8 3.5 fusion.66
  464.3 7.6 %all-to-all-done.5 = bf16[8,512,128]{1,2,0:T(8,128)(2,1)} async-done(((bf16[8,512,128]{1,2,0:T(8,128)(2,1)}), bf16[8,512,128]{1,2,0:T(8,128)(2,1)}, u32[]{:S(2)}, u32[]{:S(2)}) %all-to-all-start.5) | async-done | bytes 1048608 | tf_op jit(solution)/shard_map/all_to_all | solution.py:195
  471.9 8.9 %multiply_reduce_fusion.1 = (f32[512]{0:T(512)S(1)}, f32[512]{0:T(512)S(1)}, f32[512,1024]{1,0:T(8,128)}) fusion(f32[1024]{0:T(1024)S(1)} %copy-done.20, f32[512]{0:T(512)S(1)} %copy-done.17, f32[512]{0:T(512)S(1)} %copy-done.15, bf16[512,1024]{1,0:T(8,128)(2,1)S(1)} %copy-done.9, bf16[1024,3072]{1,0:T(8,128)(2,1)} %param.13, ...), kind=kOutput, calls=%fused_computation.91 | convolution fusion | flops 3234331648 | bytes 12595200 | tf_op jit(solution)/shard_map/dot_general | solution.py:200
  480.8 5.8 fusion.67
  486.6 6.0 pad_maximum_fusion
  492.7 130.1 %all-reduce.1 = bf16[1024,4096]{1,0:T(8,128)(2,1)} all-reduce(f32[1024,4096]{1,0:T(8,128)} %pad_maximum_fusion), channel_id=1, replica_groups=mesh['dp'=16,'seq'=8] {'dp','seq'}, use_global_device_ids=true, to_apply=%region_11.12 | all-reduce | flops 4194304 | bytes 25165824 | tf_op jit(solution)/shard_map/psum | solution.py:209
  (386 shorter events, 252.1 us)
Async XLA Ops:
  0.6 60.2 %copy-start = (bf16[1024,1024]{1,0:T(8,128)(2,1)S(1)}, bf16[1024,1024]{1,0:T(8,128)(2,1)}, u32[]{:S(2)}) copy-start(bf16[1024,1024]{1,0:T(8,128)(2,1)} %param.14) | copy-start | bytes 6291460
  0.6 3.3 copy-start.8
  0.7 3.3 copy-start.19
  2.3 8.4 %copy-start.14 = (f32[512]{0:T(512)}, f32[512]{0:T(512)S(1)}, u32[]{:S(2)}) copy-start(f32[512]{0:T(512)S(1)} %broadcast_multiply_fusion.2) | copy-start | bytes 6148
  3.9 6.7 %copy-start.16 = (f32[512]{0:T(512)}, f32[512]{0:T(512)S(1)}, u32[]{:S(2)}) copy-start(f32[512]{0:T(512)S(1)} %add_rsqrt_fusion) | copy-start | bytes 6148
  13.7 21.4 %all-to-all-start.1 = ((bf16[512,8,128]{0,2,1:T(8,128)(2,1)}), bf16[512,8,128]{0,2,1:T(8,128)(2,1)S(1)}, u32[]{:S(2)}, u32[]{:S(2)}) async-start(bf16[512,8,128]{0,2,1:T(8,128)(2,1)} %bitcast.208), calls=%async_computation.1 | async-start | bytes 2097152 | tf_op jit(solution)/shard_map/all_to_all | solution.py:167
  35.0 20.2 %all-to-all-start = ((bf16[512,8,128]{0,2,1:T(8,128)(2,1)}), bf16[512,8,128]{0,2,1:T(8,128)(2,1)}, u32[]{:S(2)}, u32[]{:S(2)}) async-start(bf16[512,8,128]{0,2,1:T(8,128)(2,1)} %bitcast.207), calls=%async_computation | async-start | bytes 2097152 | tf_op jit(solution)/shard_map/all_to_all | solution.py:166
  39.3 20.2 %copy-start.18 = (s32[1,32,8]{1,2,0:T(8,128)S(1)}, s32[1,32,8]{1,2,0:T(8,128)}, u32[]{:S(2)}) copy-start(s32[1,32,8]{1,2,0:T(8,128)} %param.15) | copy-start | bytes 3076
  39.3 20.8 %copy-start.21 = (s32[1,32]{1,0:T(1,128)S(1)}, s32[1,32]{1,0:T(1,128)}, u32[]{:S(2)}) copy-start(s32[1,32]{1,0:T(1,128)} %param.16) | copy-start | bytes 388
  55.2 31.0 %all-to-all-start.2 = ((bf16[512,8,128]{0,2,1:T(8,128)(2,1)}), bf16[512,8,128]{0,2,1:T(8,128)(2,1)}, u32[]{:S(2)}, u32[]{:S(2)}) async-start(bf16[512,8,128]{0,2,1:T(8,128)(2,1)} %bitcast.206), calls=%async_computation.2 | async-start | bytes 2097152 | tf_op jit(solution)/shard_map/all_to_all | solution.py:165
  86.2 69.1 %all-to-all-start.4 = ((bf16[512,8,128]{0,2,1:T(8,128)(2,1)}), bf16[512,8,128]{0,2,1:T(8,128)(2,1)}, u32[]{:S(2)}, u32[]{:S(2)}) async-start(bf16[512,8,128]{0,2,1:T(8,128)(2,1)} %bitcast.9), calls=%async_computation.4 | async-start | bytes 2097152 | tf_op jit(solution)/shard_map/all_to_all | solution.py:182
  155.3 255.3 %all-to-all-start.3 = ((bf16[8,512,128]{1,2,0:T(8,128)(2,1)}), bf16[8,512,128]{1,2,0:T(8,128)(2,1)}, u32[]{:S(2)}, u32[]{:S(2)}) async-start(bf16[8,512,128]{1,2,0:T(8,128)(2,1)} %all_to_all.109), calls=%async_computation.3 | async-start | bytes 2097152 | tf_op jit(solution)/shard_map/all_to_all | solution.py:175
  174.0 3.5 copy-start.7
  182.9 5.5 copy-start.4
  189.9 3.5 copy-start.2
  203.4 3.5 copy-start.7
  205.7 2.5 copy-start.3
  212.2 6.1 copy-start.4
  219.9 3.5 copy-start.2
  233.3 3.5 copy-start.7
  242.1 6.1 copy-start.4
  249.8 3.5 copy-start.2
  263.2 3.5 copy-start.7
  272.0 6.1 copy-start.4
  279.7 3.5 copy-start.2
  293.1 3.5 copy-start.7
  302.0 6.1 copy-start.4
  309.7 3.5 copy-start.2
  323.1 3.5 copy-start.7
  331.9 6.1 copy-start.4
  339.6 3.5 copy-start.2
  353.0 3.5 copy-start.7
  361.8 6.1 copy-start.4
  369.5 3.5 copy-start.2
  382.9 3.5 copy-start.7
  391.8 6.1 copy-start.4
  399.4 3.5 copy-start.2
  410.6 20.9 %all-to-all-start.7 = ((bf16[8,512,128]{1,2,0:T(8,128)(2,1)}), bf16[8,512,128]{1,2,0:T(8,128)(2,1)}, u32[]{:S(2)}, u32[]{:S(2)}) async-start(bf16[8,512,128]{1,2,0:T(8,128)(2,1)} %copy.80), calls=%async_computation.7 | async-start | bytes 2097152 | tf_op jit(solution)/shard_map/all_to_all | solution.py:197
  418.7 17.1 %copy-start.10 = (bf16[8,4,128,2,64]{2,1,4,3,0:T(4,128)(2,1)S(1)}, bf16[8,4,128,2,64]{2,1,4,3,0:T(4,128)(2,1)}, u32[]{:S(2)}) copy-start(bf16[8,4,128,2,64]{2,1,4,3,0:T(4,128)(2,1)} %get-tuple-element.113) | copy-start | bytes 3145732
  431.5 20.2 %all-to-all-start.6 = ((bf16[8,512,128]{1,2,0:T(8,128)(2,1)}), bf16[8,512,128]{1,2,0:T(8,128)(2,1)}, u32[]{:S(2)}, u32[]{:S(2)}) async-start(bf16[8,512,128]{1,2,0:T(8,128)(2,1)} %copy.79), calls=%async_computation.6 | async-start | bytes 2097152 | tf_op jit(solution)/shard_map/all_to_all | solution.py:196
  451.7 20.2 %all-to-all-start.5 = ((bf16[8,512,128]{1,2,0:T(8,128)(2,1)}), bf16[8,512,128]{1,2,0:T(8,128)(2,1)}, u32[]{:S(2)}, u32[]{:S(2)}) async-start(bf16[8,512,128]{1,2,0:T(8,128)(2,1)} %all_to_all.116), calls=%async_computation.5 | async-start | bytes 2097152 | tf_op jit(solution)/shard_map/all_to_all | solution.py:195
  456.0 4.8 copy-start.9
  460.8 11.1 %copy-start.15 = (f32[512]{0:T(512)S(1)}, f32[512]{0:T(512)}, u32[]{:S(2)}) copy-start(f32[512]{0:T(512)} %copy-done.14) | copy-start | bytes 6148
  460.8 11.1 %copy-start.17 = (f32[512]{0:T(512)S(1)}, f32[512]{0:T(512)}, u32[]{:S(2)}) copy-start(f32[512]{0:T(512)} %copy-done.16) | copy-start | bytes 6148
  460.8 11.1 %copy-start.20 = (f32[1024]{0:T(1024)S(1)}, f32[1024]{0:T(1024)}, u32[]{:S(2)}) copy-start(f32[1024]{0:T(1024)} %param.12) | copy-start | bytes 12292
  480.8 5.8 copy-start.11
  622.8 3.1 copy-start.12
  622.8 3.1 copy-start.13
  (31 other events, 53.9 us)
where the time goes:
time: 637 us; the launch traced here: 628 us
  matrix products  231 us (36%)
  local copies, waits for them, and re-layouts  138 us (22%)
  blocking collectives  130 us (20%)
  waiting for transfers between devices  59.9 us (9%)
  starting transfers between devices  37.2 us (6%)
  other arithmetic  28.9 us (5%)
    psum x1, blocking collectives, body(): lax.psum(jnp.concatenate([contract_rows(normed, grad_mixed), contract_row...  130 us
    dot_general x8, matrix products, backward_block_step(): jnp.einsum('gsc,gskhd->ckhd', selector, key_pairs, precision=lax.Precisio...  48.1 us
    while x120, local copies, waits for them, and re-layouts  42.8 us
    dot_general x16, matrix products, select_blocks(): jnp.einsum('gsc,cf->gsf', onehot, table, preferred_element_type=jnp.float32)  37.4 us
    slice x16, local copies, waits for them, and re-layouts, select_blocks(): return (picked[..., :HD], picked[..., HD:])  31.4 us
    dot_general x8, matrix products, backward_block_step(): jnp.einsum('gsc,gskhd->ckhd', selector, value_pairs, precision=lax.Precis...  28.1 us
    dot_general x8, matrix products, backward_block_step(): jnp.einsum('ghqsk,gqhd->gskhd', score_grad, query_g, preferred_element_ty...  21.4 us
    dot_general x8, matrix products, backward_block_step(): jnp.einsum('gqhd,gskhd->ghqsk', query_g, key_g, preferred_element_type=jn...  18.3 us
  transfers between devices with their start and end apart: 8, of which 5 were waited for; matrix products, arithmetic and copies ran while one was open for 54% of the time, Pallas kernels for 0%

commit v1 on v0

--- a/solution.py
+++ b/solution.py
@@ -207,10 +207,13 @@
         cotan.astype(jnp.float32) + inverse * (gained - mean_one - scaled * mean_two)
     ).astype(jnp.bfloat16)
     summed = lax.psum(
-        jnp.concatenate(
-            [contract_rows(normed, grad_mixed), contract_rows(attended, cotan)], axis=1
+        lax.psum(
+            jnp.concatenate(
+                [contract_rows(normed, grad_mixed), contract_rows(attended, cotan)], axis=1
+            ),
+            "seq",
         ),
-        ("dp", "seq"),
+        "dp",
     )
     shard_rows = model_width // seq_count
     own_rows = lax.dynamic_slice_in_dim(summed, lax.axis_index("seq") * shard_rows, shard_rows, 0)

time: 637 us -> 1060 us (1.66)
  blocking collectives: 130 us -> 363 us
  waiting for transfers between devices: 59.9 us -> 233 us
  between operations: 1.36 us -> 14.6 us
    psum x1, blocking collectives: 130 us -> 363 us  [body(): lax.psum(lax.psum(jnp.concatenate([contract_rows(normed, grad_mixed), con...]
    psum x0 -> x1, waiting for transfers between devices: none -> 170 us  [body(): lax.psum(jnp.concatenate([contract_rows(normed, grad_mixed), contract_row...]
  transfers between devices with their start and end apart: 8 -> 9, of which waited for: 5 -> 6; matrix products, arithmetic and copies ran while one was open for 54% -> 33% of each run, Pallas kernels for 0% -> 0%
where the time goes in v1:
time: 1060 us; the launch traced here: 1050 us
  blocking collectives  363 us (34%)
  waiting for transfers between devices  233 us (22%)
  matrix products  230 us (22%)
  local copies, waits for them, and re-layouts  138 us (13%)
  starting transfers between devices  37.2 us (4%)
  other arithmetic  28.9 us (3%)
  between operations  14.6 us (1%)
    psum x1, blocking collectives, body(): lax.psum(lax.psum(jnp.concatenate([contract_rows(normed, grad_mixed), con...  363 us
    psum x1, waiting for transfers between devices, body(): lax.psum(jnp.concatenate([contract_rows(normed, grad_mixed), contract_row...  170 us
    dot_general x8, matrix products, backward_block_step(): jnp.einsum('gsc,gskhd->ckhd', selector, key_pairs, precision=lax.Precisio...  48.2 us
    while x120, local copies, waits for them, and re-layouts  42.8 us
    dot_general x16, matrix products, select_blocks(): jnp.einsum('gsc,cf->gsf', onehot, table, preferred_element_type=jnp.float32)  37.4 us
    slice x16, local copies, waits for them, and re-layouts, select_blocks(): return (picked[..., :HD], picked[..., HD:])  31.5 us
    dot_general x8, matrix products, backward_block_step(): jnp.einsum('gsc,gskhd->ckhd', selector, value_pairs, precision=lax.Precis...  28.1 us
    dot_general x8, matrix products, backward_block_step(): jnp.einsum('ghqsk,gqhd->gskhd', score_grad, query_g, preferred_element_ty...  21.4 us
  transfers between devices with their start and end apart: 9, of which 6 were waited for; matrix products, arithmetic and copies ran while one was open for 33% of the time, Pallas kernels for 0%

profile of v1, /device:TPU:0, one launch (start us, length us, event | category | flops | bytes accessed | tf_op | source)
XLA Modules:
  0.0 1046.0 jit_solution(2518111499293829909)
XLA Ops:
  10.5 6.7 convolution_convert_fusion.2
  20.2 5.4 all-to-all-start.1
  27.9 13.7 %all-to-all-done.1 = bf16[512,8,128]{0,2,1:T(8,128)(2,1)S(1)} async-done(((bf16[512,8,128]{0,2,1:T(8,128)(2,1)}), bf16[512,8,128]{0,2,1:T(8,128)(2,1)S(1)}, u32[]{:S(2)}, u32[]{:S(2)}) %all-to-all-start.1) | async-done | bytes 1048608 | tf_op jit(solution)/shard_map/all_to_all | solution.py:167
  41.6 4.2 all-to-all-start
  48.1 13.7 %all-to-all-done = bf16[512,8,128]{0,2,1:T(8,128)(2,1)} async-done(((bf16[512,8,128]{0,2,1:T(8,128)(2,1)}), bf16[512,8,128]{0,2,1:T(8,128)(2,1)}, u32[]{:S(2)}, u32[]{:S(2)}) %all-to-all-start) | async-done | bytes 1048608 | tf_op jit(solution)/shard_map/all_to_all | solution.py:166
  61.8 4.2 all-to-all-start.2
  67.4 3.5 convolution_convert_fusion.3
  80.5 3.1 pad_maximum_fusion.2
  83.5 4.7 copy.69
  88.3 4.5 reshape.177
  92.8 5.2 all-to-all-start.4
  101.0 59.5 %while.28 = (s32[]{:T(128)}, bf16[8,4,128,2,64]{2,1,4,3,0:T(4,128)(2,1)S(1)}, f32[8,4,2,128]{3,2,1,0:T(2,128)S(1)}, s32[8,4,8]{2,1,0:T(4,128)S(1)}, bf16[32,3276...) while((s32[]{:T(128)}, ...), condition=%wide.region_5.6_spmd.clone, body=%wide.region_2.5_spmd.clone.sunk | while | flops 348192800 | bytes 23626400 | solution.py:75
  161.8 4.8 all-to-all-start.3
  172.1 239.4 %while.29 = (s32[]{:T(128)}, f32[32,128,2,64]{1,0,3,2:T(8,128)}, f32[32,128,2,64]{1,0,3,2:T(8,128)}, bf16[8,4,128,2,64]{2,1,4,3,0:T(4,128)(2,1)}, s32[8,4,8]{2,1...) while((s32[]{:T(128)}, f32[32,128,2,64]{1,0,3,2:T(8,128)}, ...), condition=%wide.region_8.9_spmd.clone, body=%wide.region_7.8_spmd.clone.sunk | while | flops 1153502208 | bytes 98731120 | solution.py:142
  174.6 3.0 fusion.129
  189.4 5.5 bitcast_add_fusion.4
  196.4 3.5 bitcast_add_fusion.5
  203.9 3.0 fusion.129
  218.7 6.1 bitcast_add_fusion.4
  226.4 3.5 bitcast_add_fusion.5
  233.9 3.0 fusion.129
  248.6 6.1 bitcast_add_fusion.4
  256.3 3.5 bitcast_add_fusion.5
  263.8 3.0 fusion.129
  278.6 6.1 bitcast_add_fusion.4
  286.3 3.5 bitcast_add_fusion.5
  308.5 6.1 bitcast_add_fusion.4
  316.2 3.5 bitcast_add_fusion.5
  338.5 6.1 bitcast_add_fusion.4
  346.2 3.5 bitcast_add_fusion.5
  368.4 6.1 bitcast_add_fusion.4
  376.1 3.5 bitcast_add_fusion.5
  383.6 3.0 fusion.129
  398.4 6.1 bitcast_add_fusion.4
  406.1 3.5 bitcast_add_fusion.5
  417.2 4.8 all-to-all-start.7
  427.9 10.2 all-to-all-done.7
  438.1 4.2 all-to-all-start.6
  443.6 14.7 %all-to-all-done.6 = bf16[8,512,128]{1,2,0:T(8,128)(2,1)} async-done(((bf16[8,512,128]{1,2,0:T(8,128)(2,1)}), bf16[8,512,128]{1,2,0:T(8,128)(2,1)}, u32[]{:S(2)}, u32[]{:S(2)}) %all-to-all-start.6) | async-done | bytes 1048608 | tf_op jit(solution)/shard_map/all_to_all | solution.py:196
  458.3 4.2 all-to-all-start.5
  462.7 4.8 fusion.76
  467.5 11.0 %all-to-all-done.5 = bf16[8,512,128]{1,2,0:T(8,128)(2,1)} async-done(((bf16[8,512,128]{1,2,0:T(8,128)(2,1)}), bf16[8,512,128]{1,2,0:T(8,128)(2,1)}, u32[]{:S(2)}, u32[]{:S(2)}) %all-to-all-start.5) | async-done | bytes 1048608 | tf_op jit(solution)/shard_map/all_to_all | solution.py:195
  478.6 5.8 fusion.67
  484.4 6.1 pad_maximum_fusion
  490.5 7.5 multiply_reduce_fusion.1
  499.8 3.5 fusion.66
  503.3 169.7 %all-reduce.3.cloned.1.call-done = f32[1024,4096]{1,0:T(8,128)} async-done(((f32[1024,4096]{1,0:T(8,128)}), f32[1024,4096]{1,0:T(8,128)}) %all-reduce.3.cloned.1.call-update) | async-done | bytes 16777232 | tf_op jit(solution)/shard_map/psum | solution.py:210
  673.0 363.0 %all-reduce.4 = bf16[1024,4096]{1,0:T(8,128)(2,1)} all-reduce(f32[1024,4096]{1,0:T(8,128)} %all-reduce.3.cloned.1.call-done), channel_id=1, replica_groups=mesh['dp'=16,'seq'=8] {'dp'}, use_global_device_ids=true, to_apply=%region_12.13 | all-reduce | flops 4194304 | bytes 25165824 | tf_op jit(solution)/shard_map/psum | solution.py:209
  (387 shorter events, 255.1 us)
Async XLA Ops:
  7.2 60.2 %copy-start = (bf16[1024,1024]{1,0:T(8,128)(2,1)S(1)}, bf16[1024,1024]{1,0:T(8,128)(2,1)}, u32[]{:S(2)}) copy-start(bf16[1024,1024]{1,0:T(8,128)(2,1)} %param.14) | copy-start | bytes 6291460
  7.2 3.3 copy-start.8
  7.2 3.3 copy-start.18
  8.8 8.4 copy-start.13
  10.5 6.7 copy-start.15
  20.2 21.4 %all-to-all-start.1 = ((bf16[512,8,128]{0,2,1:T(8,128)(2,1)}), bf16[512,8,128]{0,2,1:T(8,128)(2,1)S(1)}, u32[]{:S(2)}, u32[]{:S(2)}) async-start(bf16[512,8,128]{0,2,1:T(8,128)(2,1)} %bitcast.208), calls=%async_computation.1 | async-start | bytes 2097152 | tf_op jit(solution)/shard_map/all_to_all | solution.py:167
  41.6 20.2 %all-to-all-start = ((bf16[512,8,128]{0,2,1:T(8,128)(2,1)}), bf16[512,8,128]{0,2,1:T(8,128)(2,1)}, u32[]{:S(2)}, u32[]{:S(2)}) async-start(bf16[512,8,128]{0,2,1:T(8,128)(2,1)} %bitcast.207), calls=%async_computation | async-start | bytes 2097152 | tf_op jit(solution)/shard_map/all_to_all | solution.py:166
  45.8 20.2 %copy-start.17 = (s32[1,32,8]{1,2,0:T(8,128)S(1)}, s32[1,32,8]{1,2,0:T(8,128)}, u32[]{:S(2)}) copy-start(s32[1,32,8]{1,2,0:T(8,128)} %param.15) | copy-start | bytes 3076
  45.8 20.8 %copy-start.20 = (s32[1,32]{1,0:T(1,128)S(1)}, s32[1,32]{1,0:T(1,128)}, u32[]{:S(2)}) copy-start(s32[1,32]{1,0:T(1,128)} %param.16) | copy-start | bytes 388
  61.8 31.0 %all-to-all-start.2 = ((bf16[512,8,128]{0,2,1:T(8,128)(2,1)}), bf16[512,8,128]{0,2,1:T(8,128)(2,1)}, u32[]{:S(2)}, u32[]{:S(2)}) async-start(bf16[512,8,128]{0,2,1:T(8,128)(2,1)} %bitcast.206), calls=%async_computation.2 | async-start | bytes 2097152 | tf_op jit(solution)/shard_map/all_to_all | solution.py:165
  92.8 69.0 %all-to-all-start.4 = ((bf16[512,8,128]{0,2,1:T(8,128)(2,1)}), bf16[512,8,128]{0,2,1:T(8,128)(2,1)}, u32[]{:S(2)}, u32[]{:S(2)}) async-start(bf16[512,8,128]{0,2,1:T(8,128)(2,1)} %bitcast.9), calls=%async_computation.4 | async-start | bytes 2097152 | tf_op jit(solution)/shard_map/all_to_all | solution.py:182
  161.8 255.5 %all-to-all-start.3 = ((bf16[8,512,128]{1,2,0:T(8,128)(2,1)}), bf16[8,512,128]{1,2,0:T(8,128)(2,1)}, u32[]{:S(2)}, u32[]{:S(2)}) async-start(bf16[8,512,128]{1,2,0:T(8,128)(2,1)} %all_to_all.109), calls=%async_computation.3 | async-start | bytes 2097152 | tf_op jit(solution)/shard_map/all_to_all | solution.py:175
  180.5 3.5 copy-start.7
  182.8 2.5 copy-start.3
  189.4 5.5 copy-start.4
  196.4 3.5 copy-start.2
  209.8 3.5 copy-start.7
  218.7 6.1 copy-start.4
  226.4 3.5 copy-start.2
  239.8 3.5 copy-start.7
  248.6 6.1 copy-start.4
  256.3 3.5 copy-start.2
  269.8 3.5 copy-start.7
  278.6 6.1 copy-start.4
  286.3 3.5 copy-start.2
  299.7 3.5 copy-start.7
  308.5 6.1 copy-start.4
  316.2 3.5 copy-start.2
  329.7 3.5 copy-start.7
  338.5 6.1 copy-start.4
  346.2 3.5 copy-start.2
  359.6 3.5 copy-start.7
  368.4 6.1 copy-start.4
  376.1 3.5 copy-start.2
  389.6 3.5 copy-start.7
  398.4 6.1 copy-start.4
  406.1 3.5 copy-start.2
  417.2 20.9 %all-to-all-start.7 = ((bf16[8,512,128]{1,2,0:T(8,128)(2,1)}), bf16[8,512,128]{1,2,0:T(8,128)(2,1)}, u32[]{:S(2)}, u32[]{:S(2)}) async-start(bf16[8,512,128]{1,2,0:T(8,128)(2,1)} %copy.80), calls=%async_computation.7 | async-start | bytes 2097152 | tf_op jit(solution)/shard_map/all_to_all | solution.py:197
  425.3 17.1 %copy-start.10 = (bf16[8,4,128,2,64]{2,1,4,3,0:T(4,128)(2,1)S(1)}, bf16[8,4,128,2,64]{2,1,4,3,0:T(4,128)(2,1)}, u32[]{:S(2)}) copy-start(bf16[8,4,128,2,64]{2,1,4,3,0:T(4,128)(2,1)} %get-tuple-element.113) | copy-start | bytes 3145732
  438.1 20.2 %all-to-all-start.6 = ((bf16[8,512,128]{1,2,0:T(8,128)(2,1)}), bf16[8,512,128]{1,2,0:T(8,128)(2,1)}, u32[]{:S(2)}, u32[]{:S(2)}) async-start(bf16[8,512,128]{1,2,0:T(8,128)(2,1)} %copy.79), calls=%async_computation.6 | async-start | bytes 2097152 | tf_op jit(solution)/shard_map/all_to_all | solution.py:196
  458.3 20.2 %all-to-all-start.5 = ((bf16[8,512,128]{1,2,0:T(8,128)(2,1)}), bf16[8,512,128]{1,2,0:T(8,128)(2,1)}, u32[]{:S(2)}, u32[]{:S(2)}) async-start(bf16[8,512,128]{1,2,0:T(8,128)(2,1)} %all_to_all.116), calls=%async_computation.5 | async-start | bytes 2097152 | tf_op jit(solution)/shard_map/all_to_all | solution.py:195
  462.6 210.4 %all-reduce.3.cloned.1.call-start = ((), (), s32[]{:S(2)}) async-start(), calls=%async_computation.8 | async-start | bytes 33554432 | tf_op jit(solution)/shard_map/psum | solution.py:210
  462.6 15.9 %copy-start.9 = (bf16[512,1024]{1,0:T(8,128)(2,1)S(1)}, bf16[512,1024]{1,0:T(8,128)(2,1)}, u32[]{:S(2)}) copy-start(bf16[512,1024]{1,0:T(8,128)(2,1)} %param.11) | copy-start | bytes 3145732
  462.6 15.9 %copy-start.14 = (f32[512]{0:T(512)S(1)}, f32[512]{0:T(512)}, u32[]{:S(2)}) copy-start(f32[512]{0:T(512)} %copy-done.13) | copy-start | bytes 6148
  462.7 15.9 %copy-start.16 = (f32[512]{0:T(512)S(1)}, f32[512]{0:T(512)}, u32[]{:S(2)}) copy-start(f32[512]{0:T(512)} %copy-done.15) | copy-start | bytes 6148
  462.7 15.9 %copy-start.19 = (f32[1024]{0:T(1024)S(1)}, f32[1024]{0:T(1024)}, u32[]{:S(2)}) copy-start(f32[1024]{0:T(1024)} %param.12) | copy-start | bytes 12292
  478.6 5.8 copy-start.11
  490.4 7.6 copy-start.12
  (31 other events, 53.9 us)
Sparse Core Ops, SparseCore 0:
  490.6 182.3 all-reduce.2
